TPU v7x, 128 devices: a whole 4x4x4 slice. The times are simulated.
128 devices in a mesh: row: 16 (over y, z_hi, core), col: 8 (over x, z_lo).
Axes of the slice: x: 4, y: 4, z: 4 (z_hi: 2, z_lo: 2; z = z_hi * 2 + z_lo), core: 2. Of those that a mesh axis runs over, the one named last changes fastest.
Arguments:
- prior_voltage: float32 [4, 2048, 4096], P(None, 'row', 'col'), may hold values from 0.5 to 1.5
- baseline_admittance: float32 [4, 2048, 4096], P(None, 'row', 'col'), may hold values from 0.5 to 2
- block_warmth: float32 [4, 512, 1024], P(None, 'row', 'col'), may hold values from 0 to 2
- interlayer_indicator: int32 [3, 2048, 4096], P(None, 'row', 'col'), may hold values 0 or 1
- feeder_indicator: int32 [4, 2048, 4096], P(None, 'row', 'col'), may hold values 0 or 1
- injected_amperes: float32 [4, 2048, 4096], P(None, 'row', 'col'), may hold values from 0.5 to 4
Outputs:
- revised_voltage: float32 [4, 2048, 4096], P(None, 'row', 'col')
- revised_warmth: float32 [4, 512, 1024], P(None, 'row', 'col')
All inputs are finite; a program needn't handle non-finite values. No bound on the sum of `interlayer_indicator` or of `feeder_indicator` on one device may be relied on, other than what follows from the above.
Results may differ from a plain program's by a relative error of at most 0.00002.
Values sent between devices are 32-bit elements; how exact they have to be, the bound alone decides.
A program may use at most 128 MiB of HBM per device.

v0:
```python
import jax
import jax.numpy as jnp
from jax import lax
from jax.sharding import PartitionSpec as P

BLOCK_REFINE = 4
SWEEPS = 3
HEAT_SWEEPS = 4


warmth_sensitivity = 0.5
via_cond = 1.0
leak_cond = 0.2
spectrum_low = 0.05
spectrum_high = 1.95
warming_weight = 0.3
layer_admittance = 1.0
drain_admittance = 1.0
heat_gain = 0.0625
interval_length = 0.12


def padded(x, sides, width):
    for axis, dim in sides:
        size, length = (lax.axis_size(axis), x.shape[dim])
        up = [(i, (i + 1) % size) for i in range(size - 1)]
        down = [(j, i) for i, j in up]
        last = lax.slice_in_dim(x, length - width, length, axis=dim)
        leading = lax.slice_in_dim(x, 0, width, axis=dim)
        before = lax.ppermute(last, axis, up)
        after = lax.ppermute(leading, axis, down)
        x = jnp.concatenate([before, x, after], axis=dim)
    return x


def cropped_array(voltage_grid, margin):
    if margin == 0:
        return voltage_grid
    return voltage_grid[
        :, margin : voltage_grid.shape[1] - margin, margin : voltage_grid.shape[2] - margin
    ]


def neighbours(voltage_grid):
    return (
        voltage_grid[:, :-2, 1:-1],
        voltage_grid[:, 2:, 1:-1],
        voltage_grid[:, 1:-1, :-2],
        voltage_grid[:, 1:-1, 2:],
    )


def planar_edges(cond_pad):
    center = cond_pad[:, 1:-1, 1:-1]
    return tuple((jnp.sqrt(center * other) for other in neighbours(cond_pad)))


def vertical(voltage_grid, vias):
    nought_value = jnp.zeros_like(voltage_grid[:1])
    return jnp.concatenate([vias * voltage_grid[1:], nought_value], 0) + jnp.concatenate(
        [nought_value, vias * voltage_grid[:-1]], 0
    )


def via_total(vias):
    nought_value = jnp.zeros_like(vias[:1])
    return jnp.concatenate([vias, nought_value], 0) + jnp.concatenate([nought_value, vias], 0)


def operate(field_pad, edges, vias, diag):
    center = field_pad[:, 1:-1, 1:-1]
    near = jnp.zeros_like(center)
    for edge, other in zip(edges, neighbours(field_pad)):
        near = near + edge * other
    return diag * center - near - vertical(center, vias)


def joule_power(field_pad, edges, vias):
    center = field_pad[:, 1:-1, 1:-1]
    total = leak_cond * center * center
    for edge, other in zip(edges, neighbours(field_pad)):
        total = total + 0.5 * edge * (center - other) ** 2
    drop = vias * (center[:-1] - center[1:]) ** 2
    nought_value = jnp.zeros_like(center[:1])
    return total + 0.5 * (
        jnp.concatenate([drop, nought_value], 0) + jnp.concatenate([nought_value, drop], 0)
    )


def warming_increment(warmth_excess, diffusivity, warmth_border, diffusivity_border, warming_load):
    energy_flow = jnp.zeros_like(warmth_excess)
    for partner_warmth, partner_diffusivity in zip(
        neighbours(warmth_border), neighbours(diffusivity_border)
    ):
        energy_flow = energy_flow + jnp.sqrt(diffusivity * partner_diffusivity) * (
            partner_warmth - warmth_excess
        )
    nought_value = jnp.zeros_like(warmth_excess[:1])
    upright_flow = layer_admittance * (
        jnp.concatenate([warmth_excess[1:] - warmth_excess[:-1], nought_value], 0)
        + jnp.concatenate([nought_value, warmth_excess[:-1] - warmth_excess[1:]], 0)
    )
    layer_total = warmth_excess.shape[0]
    upper_layer = (
        lax.broadcasted_iota(jnp.int32, (layer_total, 1, 1), 0) == layer_total - 1
    ).astype(jnp.float32)
    return warmth_excess + interval_length * (
        energy_flow + upright_flow + warming_load - drain_admittance * upper_layer * warmth_excess
    )


def inside_mask(rows, cols, row_first, col_first, row_total, col_total):
    row_ids = lax.broadcasted_iota(jnp.int32, (1, rows, cols), 1) + row_first
    col_ids = lax.broadcasted_iota(jnp.int32, (1, rows, cols), 2) + col_first
    inside = (row_ids >= 0) & (row_ids < row_total) & (col_ids >= 0) & (col_ids < col_total)
    return inside.astype(jnp.float32)


def masked_kappa(warmth_border, inside):
    return jnp.exp(-warming_weight * warmth_border) * inside


def rim(voltage_grid):
    return padded(voltage_grid, (("row", 1), ("col", 2)), 1)


def on_device(
    prior_voltage,
    baseline_admittance,
    block_warmth,
    interlayer_indicator,
    feeder_indicator,
    injected_amperes,
):
    warmth_on_points = jnp.repeat(
        jnp.repeat(block_warmth, BLOCK_REFINE, axis=1), BLOCK_REFINE, axis=2
    )
    admittance = baseline_admittance * jnp.exp(-warmth_sensitivity * warmth_on_points)
    vias = via_cond * interlayer_indicator.astype(jnp.float32)
    inject = feeder_indicator.astype(jnp.float32) * injected_amperes
    width = 1
    field_pad, cond_pad = (
        padded(prior_voltage, (("row", 1), ("col", 2)), 1),
        padded(admittance, (("row", 1), ("col", 2)), 1),
    )
    inject_pad, vias_pad = (inject, vias)
    side_margin = 0
    edge_margin = width - 1
    edges_all = planar_edges(cond_pad)
    diag_all = (
        leak_cond
        + edges_all[0]
        + edges_all[1]
        + edges_all[2]
        + edges_all[3]
        + via_total(cropped_array(vias_pad, side_margin - edge_margin))
    )

    def pieces(want):
        edges = tuple((cropped_array(edge, edge_margin - want) for edge in edges_all))
        return (
            edges,
            cropped_array(vias_pad, side_margin - want),
            cropped_array(diag_all, edge_margin - want),
            cropped_array(inject_pad, side_margin - want),
        )

    center_c = 0.5 * (spectrum_high + spectrum_low)
    half = 0.5 * (spectrum_high - spectrum_low)
    sigma = center_c / half
    rho = 1.0 / sigma
    field_margin = width
    out_margin = field_margin - 1
    edges, vias_m, diag_m, inject_m = pieces(out_margin)
    resid = inject_m - operate(field_pad, edges, vias_m, diag_m)
    step = resid / (diag_m * center_c)
    step_margin = out_margin
    voltage_grid = field_pad
    for sweep in range(SWEEPS):
        voltage_grid = cropped_array(voltage_grid, field_margin - step_margin) + step
        field_margin = step_margin
        if sweep < SWEEPS - 1:
            voltage_grid = rim(voltage_grid)
            field_margin = 1
            out_margin = field_margin - 1
            edges, vias_m, diag_m, inject_m = pieces(out_margin)
            resid = inject_m - operate(voltage_grid, edges, vias_m, diag_m)
            rho_new = 1.0 / (2.0 * sigma - rho)
            step = rho_new * rho * cropped_array(
                step, step_margin - out_margin
            ) + 2.0 * rho_new / half * (resid / diag_m)
            step_margin = out_margin
            rho = rho_new
    revised_voltage = cropped_array(voltage_grid, field_margin)
    voltage_grid = rim(voltage_grid)
    field_margin = 1
    edges, vias_m, diag_m, inject_m = pieces(0)
    power = joule_power(cropped_array(voltage_grid, field_margin - 1), edges, vias_m)
    layer_total, rows, cols = power.shape
    warming_load = (
        power.reshape(
            layer_total, rows // BLOCK_REFINE, BLOCK_REFINE, cols // BLOCK_REFINE, BLOCK_REFINE
        ).sum(axis=(2, 4))
        * heat_gain
    )
    heated_heightwise = block_warmth.shape[1]
    heated_widthwise = block_warmth.shape[2]
    row_total = heated_heightwise * lax.axis_size("row")
    col_total = heated_widthwise * lax.axis_size("col")
    leading_line_offset = lax.axis_index("row") * heated_heightwise
    col_start = lax.axis_index("col") * heated_widthwise
    inside = inside_mask(
        heated_heightwise + 2,
        heated_widthwise + 2,
        leading_line_offset - 1,
        col_start - 1,
        row_total,
        col_total,
    )
    warmth_excess = block_warmth
    for sweep in range(HEAT_SWEEPS):
        warmth_border = padded(warmth_excess, (("row", 1), ("col", 2)), 1)
        diffusivity_border = masked_kappa(warmth_border, inside)
        warmth_excess = warming_increment(
            warmth_excess,
            cropped_array(diffusivity_border, 1),
            warmth_border,
            diffusivity_border,
            warming_load,
        )
    return (revised_voltage, warmth_excess)


def solution(mesh):
    placed = (
        P(None, "row", "col"),
        P(None, "row", "col"),
        P(None, "row", "col"),
        P(None, "row", "col"),
        P(None, "row", "col"),
        P(None, "row", "col"),
    )
    return jax.shard_map(
        on_device,
        mesh=mesh,
        in_specs=placed,
        out_specs=(P(None, "row", "col"), P(None, "row", "col")),
        check_vma=False,
    )
```

profile of v0, /device:TPU:1, one launch (start us, length us, event | category | flops | bytes accessed | tf_op | source)
XLA Modules:
  0.0 275.3 jit_solution(1779275655002841198)
XLA Ops:
  4.3 6.9 %collective-permute-start = (f32[4,1,512]{2,0,1:T(4,128)S(1)}, f32[4,1,512]{2,0,1:T(4,128)S(1)}, u32[]{:S(2)}, u32[]{:S(2)}) collective-permute-start(f32[4,1,512]{2,0,1:T(4,128)S(1)} %copy.44), channel_id=1, source_target_pairs={{0,8},{8,16},{16,24},{24,32},{32,40},{40,48},{48,56},{56,64},{64,7... | collective-permute-start | bytes 24584 | tf_op jit(solution)/shard_map/ppermute | solution.py:30
  14.4 5.1 %collective-permute-start.4 = (f32[4,1,512]{2,0,1:T(4,128)S(1)}, f32[4,1,512]{2,0,1:T(4,128)S(1)}, u32[]{:S(2)}, u32[]{:S(2)}) collective-permute-start(f32[4,1,512]{2,0,1:T(4,128)S(1)} %copy.84), channel_id=1, source_target_pairs={{0,8},{8,16},{16,24},{24,32},{32,40},{40,48},{48,56},{56,64},{64,7... | collective-permute-start | bytes 24584 | tf_op jit(solution)/shard_map/ppermute | solution.py:30
  22.2 5.1 %collective-permute-start.16 = (f32[4,1,128]{2,1,0:T(1,128)S(1)}, f32[4,1,128]{2,1,0:T(1,128)S(1)}, u32[]{:S(2)}, u32[]{:S(2)}) collective-permute-start(f32[4,1,128]{2,1,0:T(1,128)S(1)} %get-tuple-element.64), channel_id=1, source_target_pairs={{0,8},{8,16},{16,24},{24,32},{32,40},{40,48},{48,56},{56,64},{64,7... | collective-permute-start | bytes 6152 | tf_op jit(solution)/shard_map/ppermute | solution.py:30
  44.5 4.2 %collective-permute-start.6 = (f32[4,130,1]{1,2,0:T(1,128)S(1)}, f32[4,130,1]{1,2,0:T(1,128)S(1)}, u32[]{:S(2)}, u32[]{:S(2)}) collective-permute-start(f32[4,130,1]{1,2,0:T(1,128)S(1)} %get-tuple-element.24), channel_id=1, source_target_pairs={{0,1},{1,2},{2,3},{3,4},{4,5},{5,6},{6,7},{8,9},{9,10},{10,11},{11... | collective-permute-start | bytes 6248 | tf_op jit(solution)/shard_map/ppermute | solution.py:30
  58.6 10.5 %fusion.151 = (f32[4,128,512]{1,2,0:T(8,128)S(1)}, f32[4,128,512]{1,2,0:T(8,128)}, f32[4,128,512]{1,2,0:T(8,128)}, f32[4,128,512]{1,2,0:T(8,128)}, f32[4,128,512]{1,2,0:T(8,128)}, /*index=5*/f32[4,128,512]{1,2,0:T(8,128)}) fusion(f32[4,128,512]{1,2,0:T(8,128)} %copy-done, f32[3,128,512]{1,2,0:T(8,128)} %get-tuple-element.31, ...), kind=kLoop, calls=%fused_computation.287 | loop fusion | flops 11010048 | bytes 12886144 | tf_op jit(solution)/shard_map/add | solution.py:180
  72.1 5.1 %collective-permute-start.8 = (f32[4,1,512]{2,0,1:T(4,128)S(1)}, f32[4,1,512]{2,0,1:T(4,128)S(1)}, u32[]{:S(2)}, u32[]{:S(2)}) collective-permute-start(f32[4,1,512]{2,0,1:T(4,128)S(1)} %copy.64), channel_id=1, source_target_pairs={{0,8},{8,16},{16,24},{24,32},{32,40},{40,48},{48,56},{56,64},{64,7... | collective-permute-start | bytes 24584 | tf_op jit(solution)/shard_map/ppermute | solution.py:30
  79.9 4.1 %collective-permute-done.9 = f32[4,1,512]{2,0,1:T(4,128)S(1)} collective-permute-done((f32[4,1,512]{2,0,1:T(4,128)S(1)}, f32[4,1,512]{2,0,1:T(4,128)S(1)}, u32[]{:S(2)}, u32[]{:S(2)}) %collective-permute-start.9) | collective-permute-done | bytes 8224 | tf_op jit(solution)/shard_map/ppermute | solution.py:31
  86.2 4.9 %collective-permute-start.10 = (f32[4,130,1]{1,2,0:T(1,128)S(1)}, f32[4,130,1]{1,2,0:T(1,128)S(1)}, u32[]{:S(2)}, u32[]{:S(2)}) collective-permute-start(f32[4,130,1]{1,2,0:T(1,128)S(1)} %get-tuple-element.20), channel_id=1, source_target_pairs={{0,1},{1,2},{2,3},{3,4},{4,5},{5,6},{6,7},{8,9},{9,10},{10,11},{11... | collective-permute-start | bytes 6248 | tf_op jit(solution)/shard_map/ppermute | solution.py:30
  92.5 3.8 %collective-permute-done.11 = f32[4,130,1]{1,2,0:T(1,128)S(1)} collective-permute-done((f32[4,130,1]{1,2,0:T(1,128)S(1)}, f32[4,130,1]{1,2,0:T(1,128)S(1)}, u32[]{:S(2)}, u32[]{:S(2)}) %collective-permute-start.11) | collective-permute-done | bytes 2112 | tf_op jit(solution)/shard_map/ppermute | solution.py:31
  96.4 6.8 %fusion.150 = (f32[4,128,512]{1,2,0:T(8,128)S(1)}, f32[4,128,512]{1,2,0:T(8,128)}) fusion(f32[4,128,512]{1,2,0:T(8,128)S(1)} %get-tuple-element.10, f32[3,128,512]{1,2,0:T(8,128)S(1)} %get-tuple-element.29, f32[3,128,512]{1,2,0:T(8,128)S(1)} %get-tuple-element.28, f32[4,128,512]{1,2,0:T(8,128)} %get-tuple-element.15, ...), kind=kLoop, calls=%fused_computation.286 | loop fusion | flops 8650752 | bytes 12865600 | tf_op jit(solution)/shard_map/add | solution.py:180
  106.0 3.1 %collective-permute-start.12 = (f32[4,1,512]{2,0,1:T(4,128)S(1)}, f32[4,1,512]{2,0,1:T(4,128)S(1)}, u32[]{:S(2)}, u32[]{:S(2)}) collective-permute-start(f32[4,1,512]{2,0,1:T(4,128)S(1)} %copy.70), channel_id=1, source_target_pairs={{0,8},{8,16},{16,24},{24,32},{32,40},{40,48},{48,56},{56,64},{64,7... | collective-permute-start | bytes 24584 | tf_op jit(solution)/shard_map/ppermute | solution.py:30
  111.5 3.9 %collective-permute-start.18 = (f32[4,34,1]{2,1,0:T(8,128)S(1)}, f32[4,34,1]{2,1,0:T(8,128)S(1)}, u32[]{:S(2)}, u32[]{:S(2)}) collective-permute-start(f32[4,34,1]{2,1,0:T(8,128)S(1)} %get-tuple-element.48), channel_id=1, source_target_pairs={{0,1},{1,2},{2,3},{3,4},{4,5},{5,6},{6,7},{8,9},{9,10},{10,11},{11... | collective-permute-start | bytes 1640 | tf_op jit(solution)/shard_map/ppermute | solution.py:30
  119.3 4.0 %collective-permute-start.14 = (f32[4,130,1]{1,2,0:T(1,128)S(1)}, f32[4,130,1]{1,2,0:T(1,128)S(1)}, u32[]{:S(2)}, u32[]{:S(2)}) collective-permute-start(f32[4,130,1]{1,2,0:T(1,128)S(1)} %get-tuple-element.18), channel_id=1, source_target_pairs={{0,1},{1,2},{2,3},{3,4},{4,5},{5,6},{6,7},{8,9},{9,10},{10,11},{11... | collective-permute-start | bytes 6248 | tf_op jit(solution)/shard_map/ppermute | solution.py:30
  124.9 2.7 collective-permute-done.15
  127.6 6.1 %add_add_fusion = f32[4,128,512]{1,2,0:T(8,128)S(1)} fusion(f32[4,128,512]{1,2,0:T(8,128)S(1)} %get-tuple-element.8, f32[4,128,512]{1,2,0:T(8,128)} %get-tuple-element.15, f32[4,130,1]{1,2,0:T(1,128)S(1)} %collective-permute-done.15, f32[4,1,512]{1,2,0:T(8,128)} %copy.73, f32[4,1,512]{1,2,0:T(8,128)} %copy-done.1, f32[4,128,512]{1,2,0:T(8,128)} %get-tuple-element.14, ...), kind=kLoop, calls=%fused_computation.99 | loop fusion | flops 8650752 | bytes 11817024 | tf_op jit(solution)/shard_map/add | solution.py:180
  136.6 7.7 %collective-permute-start.20 = (f32[4,1,512]{2,0,1:T(4,128)S(1)}, f32[4,1,512]{2,0,1:T(4,128)S(1)}, u32[]{:S(2)}, u32[]{:S(2)}) collective-permute-start(f32[4,1,512]{2,0,1:T(4,128)S(1)} %copy.76), channel_id=1, source_target_pairs={{0,8},{8,16},{16,24},{24,32},{32,40},{40,48},{48,56},{56,64},{64,7... | collective-permute-start | bytes 24584 | tf_op jit(solution)/shard_map/ppermute | solution.py:30
  147.2 4.0 %collective-permute-done.21 = f32[4,1,512]{2,0,1:T(4,128)S(1)} collective-permute-done((f32[4,1,512]{2,0,1:T(4,128)S(1)}, f32[4,1,512]{2,0,1:T(4,128)S(1)}, u32[]{:S(2)}, u32[]{:S(2)}) %collective-permute-start.21) | collective-permute-done | bytes 8224 | tf_op jit(solution)/shard_map/ppermute | solution.py:31
  153.3 2.9 %collective-permute-start.22 = (f32[4,130,1]{1,2,0:T(1,128)S(1)}, f32[4,130,1]{1,2,0:T(1,128)S(1)}, u32[]{:S(2)}, u32[]{:S(2)}) collective-permute-start(f32[4,130,1]{1,2,0:T(1,128)S(1)} %get-tuple-element.16), channel_id=1, source_target_pairs={{0,1},{1,2},{2,3},{3,4},{4,5},{5,6},{6,7},{8,9},{9,10},{10,11},{11... | collective-permute-start | bytes 6248 | tf_op jit(solution)/shard_map/ppermute | solution.py:30
  157.6 2.9 %collective-permute-done.23 = f32[4,130,1]{1,2,0:T(1,128)S(1)} collective-permute-done((f32[4,130,1]{1,2,0:T(1,128)S(1)}, f32[4,130,1]{1,2,0:T(1,128)S(1)}, u32[]{:S(2)}, u32[]{:S(2)}) %collective-permute-start.23) | collective-permute-done | bytes 2112 | tf_op jit(solution)/shard_map/ppermute | solution.py:31
  160.5 3.8 %fusion.4 = f32[4,128,512]{1,2,0:T(8,128)S(1)} fusion(f32[4,128,512]{1,2,0:T(8,128)S(1)} %add_add_fusion, f32[4,130,1]{1,2,0:T(1,128)S(1)} %collective-permute-done.23, f32[4,1,512]{1,2,0:T(8,128)} %copy.79, f32[4,1,512]{1,2,0:T(8,128)S(1)} %copy.77, f32[4,130,1]{1,2,0:T(1,128)S(1)} %collective-permute-done.22, f32[3,128,512]{1,2,0:T(8,128)S(1)} %fusion.59, ...), kind=kLoop, calls=%fused_computation.5 | loop fusion | flops 8650752 | bytes 7098432 | tf_op jit(solution)/shard_map/add | solution.py:85
  164.7 35.9 %reshape.68 = f32[4,32,4,128,4]{4,3,2,1,0:T(8,128)} reshape(f32[4,128,512]{2,1,0:T(8,128)S(1)} %copy.82) | data formatting | bytes 2097152 | tf_op jit(solution)/shard_map/reshape | solution.py:201
  200.6 12.2 %reduce_sum.9 = f32[4,32,128]{2,1,0:T(8,128)S(1)} reduce(f32[4,32,4,128,4]{4,3,2,1,0:T(8,128)} %reshape.68, f32[]{:T(128)} %constant.5.clone.1), dimensions={2,4}, to_apply=%region_0.0 | reduce | flops 245760 | bytes 1114116 | tf_op jit(solution)/shard_map/reduce_sum | solution.py:203
  213.1 5.9 %collective-permute-start.24 = (f32[4,1,128]{2,1,0:T(1,128)S(1)}, f32[4,1,128]{2,1,0:T(1,128)S(1)}, u32[]{:S(2)}, u32[]{:S(2)}) collective-permute-start(f32[4,1,128]{2,1,0:T(1,128)S(1)} %get-tuple-element.60), channel_id=1, source_target_pairs={{0,8},{8,16},{16,24},{24,32},{32,40},{40,48},{48,56},{56,64},{64,7... | collective-permute-start | bytes 6152 | tf_op jit(solution)/shard_map/ppermute | solution.py:30
  221.0 4.6 %collective-permute-done.25 = f32[4,1,128]{2,1,0:T(1,128)S(1)} collective-permute-done((f32[4,1,128]{2,1,0:T(1,128)S(1)}, f32[4,1,128]{2,1,0:T(1,128)S(1)}, u32[]{:S(2)}, u32[]{:S(2)}) %collective-permute-start.25) | collective-permute-done | bytes 2080 | tf_op jit(solution)/shard_map/ppermute | solution.py:31
  229.6 4.1 %collective-permute-done.27 = f32[4,34,1]{2,1,0:T(8,128)S(1)} collective-permute-done((f32[4,34,1]{2,1,0:T(8,128)S(1)}, f32[4,34,1]{2,1,0:T(8,128)S(1)}, u32[]{:S(2)}, u32[]{:S(2)}) %collective-permute-start.27) | collective-permute-done | bytes 576 | tf_op jit(solution)/shard_map/ppermute | solution.py:31
  234.1 5.0 %collective-permute-start.28 = (f32[4,1,128]{2,1,0:T(1,128)S(1)}, f32[4,1,128]{2,1,0:T(1,128)S(1)}, u32[]{:S(2)}, u32[]{:S(2)}) collective-permute-start(f32[4,1,128]{2,1,0:T(1,128)S(1)} %get-tuple-element.56), channel_id=1, source_target_pairs={{0,8},{8,16},{16,24},{24,32},{32,40},{40,48},{48,56},{56,64},{64,7... | collective-permute-start | bytes 6152 | tf_op jit(solution)/shard_map/ppermute | solution.py:30
  241.1 4.5 %collective-permute-done.29 = f32[4,1,128]{2,1,0:T(1,128)S(1)} collective-permute-done((f32[4,1,128]{2,1,0:T(1,128)S(1)}, f32[4,1,128]{2,1,0:T(1,128)S(1)}, u32[]{:S(2)}, u32[]{:S(2)}) %collective-permute-start.29) | collective-permute-done | bytes 2080 | tf_op jit(solution)/shard_map/ppermute | solution.py:31
  249.4 5.0 %collective-permute-done.31 = f32[4,34,1]{2,1,0:T(8,128)S(1)} collective-permute-done((f32[4,34,1]{2,1,0:T(8,128)S(1)}, f32[4,34,1]{2,1,0:T(8,128)S(1)}, u32[]{:S(2)}, u32[]{:S(2)}) %collective-permute-start.31) | collective-permute-done | bytes 576 | tf_op jit(solution)/shard_map/ppermute | solution.py:31
  254.8 4.1 %collective-permute-start.32 = (f32[4,1,128]{2,1,0:T(1,128)S(1)}, f32[4,1,128]{2,1,0:T(1,128)S(1)}, u32[]{:S(2)}, u32[]{:S(2)}) collective-permute-start(f32[4,1,128]{2,1,0:T(1,128)S(1)} %get-tuple-element.52), channel_id=1, source_target_pairs={{0,8},{8,16},{16,24},{24,32},{32,40},{40,48},{48,56},{56,64},{64,7... | collective-permute-start | bytes 6152 | tf_op jit(solution)/shard_map/ppermute | solution.py:30
  262.2 3.2 %collective-permute-done.33 = f32[4,1,128]{2,1,0:T(1,128)S(1)} collective-permute-done((f32[4,1,128]{2,1,0:T(1,128)S(1)}, f32[4,1,128]{2,1,0:T(1,128)S(1)}, u32[]{:S(2)}, u32[]{:S(2)}) %collective-permute-start.33) | collective-permute-done | bytes 2080 | tf_op jit(solution)/shard_map/ppermute | solution.py:31
  265.6 2.9 %collective-permute-start.34 = (f32[4,34,1]{2,1,0:T(8,128)S(1)}, f32[4,34,1]{2,1,0:T(8,128)S(1)}, u32[]{:S(2)}, u32[]{:S(2)}) collective-permute-start(f32[4,34,1]{2,1,0:T(8,128)S(1)} %get-tuple-element.42), channel_id=1, source_target_pairs={{0,1},{1,2},{2,3},{3,4},{4,5},{5,6},{6,7},{8,9},{9,10},{10,11},{11... | collective-permute-start | bytes 1640 | tf_op jit(solution)/shard_map/ppermute | solution.py:30
  270.0 4.3 %collective-permute-done.35 = f32[4,34,1]{2,1,0:T(8,128)S(1)} collective-permute-done((f32[4,34,1]{2,1,0:T(8,128)S(1)}, f32[4,34,1]{2,1,0:T(8,128)S(1)}, u32[]{:S(2)}, u32[]{:S(2)}) %collective-permute-start.35) | collective-permute-done | bytes 576 | tf_op jit(solution)/shard_map/ppermute | solution.py:31
  (137 shorter events, 84.1 us)
Async XLA Ops:
  4.3 29.0 %collective-permute-start = (f32[4,1,512]{2,0,1:T(4,128)S(1)}, f32[4,1,512]{2,0,1:T(4,128)S(1)}, u32[]{:S(2)}, u32[]{:S(2)}) collective-permute-start(f32[4,1,512]{2,0,1:T(4,128)S(1)} %copy.44), channel_id=1, source_target_pairs={{0,8},{8,16},{16,24},{24,32},{32,40},{40,48},{48,56},{56,64},{64,7... | collective-permute-start | bytes 24584 | tf_op jit(solution)/shard_map/ppermute | solution.py:30
  11.6 23.1 %collective-permute-start.1 = (f32[4,1,512]{2,0,1:T(4,128)S(1)}, f32[4,1,512]{2,0,1:T(4,128)S(1)}, u32[]{:S(2)}, u32[]{:S(2)}) collective-permute-start(f32[4,1,512]{2,0,1:T(4,128)S(1)} %copy.46), channel_id=1, source_target_pairs={{8,0},{16,8},{24,16},{32,24},{40,32},{48,40},{56,48},{64,56},{72,6... | collective-permute-start | bytes 24584 | tf_op jit(solution)/shard_map/ppermute | solution.py:31
  14.4 26.4 %collective-permute-start.4 = (f32[4,1,512]{2,0,1:T(4,128)S(1)}, f32[4,1,512]{2,0,1:T(4,128)S(1)}, u32[]{:S(2)}, u32[]{:S(2)}) collective-permute-start(f32[4,1,512]{2,0,1:T(4,128)S(1)} %copy.84), channel_id=1, source_target_pairs={{0,8},{8,16},{16,24},{24,32},{32,40},{40,48},{48,56},{56,64},{64,7... | collective-permute-start | bytes 24584 | tf_op jit(solution)/shard_map/ppermute | solution.py:30
  19.6 22.7 %collective-permute-start.5 = (f32[4,1,512]{2,0,1:T(4,128)S(1)}, f32[4,1,512]{2,0,1:T(4,128)S(1)}, u32[]{:S(2)}, u32[]{:S(2)}) collective-permute-start(f32[4,1,512]{2,0,1:T(4,128)S(1)} %copy.85), channel_id=1, source_target_pairs={{8,0},{16,8},{24,16},{32,24},{40,32},{48,40},{56,48},{64,56},{72,6... | collective-permute-start | bytes 24584 | tf_op jit(solution)/shard_map/ppermute | solution.py:31
  22.2 57.3 %collective-permute-start.16 = (f32[4,1,128]{2,1,0:T(1,128)S(1)}, f32[4,1,128]{2,1,0:T(1,128)S(1)}, u32[]{:S(2)}, u32[]{:S(2)}) collective-permute-start(f32[4,1,128]{2,1,0:T(1,128)S(1)} %get-tuple-element.64), channel_id=1, source_target_pairs={{0,8},{8,16},{16,24},{24,32},{32,40},{40,48},{48,56},{56,64},{64,7... | collective-permute-start | bytes 6152 | tf_op jit(solution)/shard_map/ppermute | solution.py:30
  36.9 19.8 %collective-permute-start.2 = (f32[4,130,1]{1,2,0:T(1,128)S(1)}, f32[4,130,1]{1,2,0:T(1,128)S(1)}, u32[]{:S(2)}, u32[]{:S(2)}) collective-permute-start(f32[4,130,1]{1,2,0:T(1,128)S(1)} %get-tuple-element.23), channel_id=1, source_target_pairs={{0,1},{1,2},{2,3},{3,4},{4,5},{5,6},{6,7},{8,9},{9,10},{10,11},{11... | collective-permute-start | bytes 6248 | tf_op jit(solution)/shard_map/ppermute | solution.py:30
  39.5 19.1 %collective-permute-start.3 = (f32[4,130,1]{1,2,0:T(1,128)S(1)}, f32[4,130,1]{1,2,0:T(1,128)S(1)}, u32[]{:S(2)}, u32[]{:S(2)}) collective-permute-start(f32[4,130,1]{1,2,0:T(1,128)S(1)} %get-tuple-element.22), channel_id=1, source_target_pairs={{1,0},{2,1},{3,2},{4,3},{5,4},{6,5},{7,6},{9,8},{10,9},{11,10},{12... | collective-permute-start | bytes 6248 | tf_op jit(solution)/shard_map/ppermute | solution.py:31
  44.5 14.1 %collective-permute-start.6 = (f32[4,130,1]{1,2,0:T(1,128)S(1)}, f32[4,130,1]{1,2,0:T(1,128)S(1)}, u32[]{:S(2)}, u32[]{:S(2)}) collective-permute-start(f32[4,130,1]{1,2,0:T(1,128)S(1)} %get-tuple-element.24), channel_id=1, source_target_pairs={{0,1},{1,2},{2,3},{3,4},{4,5},{5,6},{6,7},{8,9},{9,10},{10,11},{11... | collective-permute-start | bytes 6248 | tf_op jit(solution)/shard_map/ppermute | solution.py:30
  48.7 9.9 %collective-permute-start.7 = (f32[4,130,1]{1,2,0:T(1,128)S(1)}, f32[4,130,1]{1,2,0:T(1,128)S(1)}, u32[]{:S(2)}, u32[]{:S(2)}) collective-permute-start(f32[4,130,1]{1,2,0:T(1,128)S(1)} %get-tuple-element.25), channel_id=1, source_target_pairs={{1,0},{2,1},{3,2},{4,3},{5,4},{6,5},{7,6},{9,8},{10,9},{11,10},{12... | collective-permute-start | bytes 6248 | tf_op jit(solution)/shard_map/ppermute | solution.py:31
  56.7 22.8 %collective-permute-start.17 = (f32[4,1,128]{2,1,0:T(1,128)S(1)}, f32[4,1,128]{2,1,0:T(1,128)S(1)}, u32[]{:S(2)}, u32[]{:S(2)}) collective-permute-start(f32[4,1,128]{2,1,0:T(1,128)S(1)} %get-tuple-element.65), channel_id=1, source_target_pairs={{8,0},{16,8},{24,16},{32,24},{40,32},{48,40},{56,48},{64,56},{72,6... | collective-permute-start | bytes 6152 | tf_op jit(solution)/shard_map/ppermute | solution.py:31
  72.1 7.5 %collective-permute-start.8 = (f32[4,1,512]{2,0,1:T(4,128)S(1)}, f32[4,1,512]{2,0,1:T(4,128)S(1)}, u32[]{:S(2)}, u32[]{:S(2)}) collective-permute-start(f32[4,1,512]{2,0,1:T(4,128)S(1)} %copy.64), channel_id=1, source_target_pairs={{0,8},{8,16},{16,24},{24,32},{32,40},{40,48},{48,56},{56,64},{64,7... | collective-permute-start | bytes 24584 | tf_op jit(solution)/shard_map/ppermute | solution.py:30
  77.5 6.5 %collective-permute-start.9 = (f32[4,1,512]{2,0,1:T(4,128)S(1)}, f32[4,1,512]{2,0,1:T(4,128)S(1)}, u32[]{:S(2)}, u32[]{:S(2)}) collective-permute-start(f32[4,1,512]{2,0,1:T(4,128)S(1)} %copy.66), channel_id=1, source_target_pairs={{8,0},{16,8},{24,16},{32,24},{40,32},{48,40},{56,48},{64,56},{72,6... | collective-permute-start | bytes 24584 | tf_op jit(solution)/shard_map/ppermute | solution.py:31
  86.2 6.3 %collective-permute-start.10 = (f32[4,130,1]{1,2,0:T(1,128)S(1)}, f32[4,130,1]{1,2,0:T(1,128)S(1)}, u32[]{:S(2)}, u32[]{:S(2)}) collective-permute-start(f32[4,130,1]{1,2,0:T(1,128)S(1)} %get-tuple-element.20), channel_id=1, source_target_pairs={{0,1},{1,2},{2,3},{3,4},{4,5},{5,6},{6,7},{8,9},{9,10},{10,11},{11... | collective-permute-start | bytes 6248 | tf_op jit(solution)/shard_map/ppermute | solution.py:30
  91.1 5.3 %collective-permute-start.11 = (f32[4,130,1]{1,2,0:T(1,128)S(1)}, f32[4,130,1]{1,2,0:T(1,128)S(1)}, u32[]{:S(2)}, u32[]{:S(2)}) collective-permute-start(f32[4,130,1]{1,2,0:T(1,128)S(1)} %get-tuple-element.21), channel_id=1, source_target_pairs={{1,0},{2,1},{3,2},{4,3},{5,4},{6,5},{7,6},{9,8},{10,9},{11,10},{12... | collective-permute-start | bytes 6248 | tf_op jit(solution)/shard_map/ppermute | solution.py:31
  106.0 10.7 %collective-permute-start.12 = (f32[4,1,512]{2,0,1:T(4,128)S(1)}, f32[4,1,512]{2,0,1:T(4,128)S(1)}, u32[]{:S(2)}, u32[]{:S(2)}) collective-permute-start(f32[4,1,512]{2,0,1:T(4,128)S(1)} %copy.70), channel_id=1, source_target_pairs={{0,8},{8,16},{16,24},{24,32},{32,40},{40,48},{48,56},{56,64},{64,7... | collective-permute-start | bytes 24584 | tf_op jit(solution)/shard_map/ppermute | solution.py:30
  109.4 7.7 %collective-permute-start.13 = (f32[4,1,512]{2,0,1:T(4,128)S(1)}, f32[4,1,512]{2,0,1:T(4,128)S(1)}, u32[]{:S(2)}, u32[]{:S(2)}) collective-permute-start(f32[4,1,512]{2,0,1:T(4,128)S(1)} %copy.72), channel_id=1, source_target_pairs={{8,0},{16,8},{24,16},{32,24},{40,32},{48,40},{56,48},{64,56},{72,6... | collective-permute-start | bytes 24584 | tf_op jit(solution)/shard_map/ppermute | solution.py:31
  111.5 35.1 %collective-permute-start.18 = (f32[4,34,1]{2,1,0:T(8,128)S(1)}, f32[4,34,1]{2,1,0:T(8,128)S(1)}, u32[]{:S(2)}, u32[]{:S(2)}) collective-permute-start(f32[4,34,1]{2,1,0:T(8,128)S(1)} %get-tuple-element.48), channel_id=1, source_target_pairs={{0,1},{1,2},{2,3},{3,4},{4,5},{5,6},{6,7},{8,9},{9,10},{10,11},{11... | collective-permute-start | bytes 1640 | tf_op jit(solution)/shard_map/ppermute | solution.py:30
  115.4 31.2 %collective-permute-start.19 = (f32[4,34,1]{2,1,0:T(8,128)S(1)}, f32[4,34,1]{2,1,0:T(8,128)S(1)}, u32[]{:S(2)}, u32[]{:S(2)}) collective-permute-start(f32[4,34,1]{2,1,0:T(8,128)S(1)} %get-tuple-element.49), channel_id=1, source_target_pairs={{1,0},{2,1},{3,2},{4,3},{5,4},{6,5},{7,6},{9,8},{10,9},{11,10},{12... | collective-permute-start | bytes 1640 | tf_op jit(solution)/shard_map/ppermute | solution.py:31
  119.3 5.6 %collective-permute-start.14 = (f32[4,130,1]{1,2,0:T(1,128)S(1)}, f32[4,130,1]{1,2,0:T(1,128)S(1)}, u32[]{:S(2)}, u32[]{:S(2)}) collective-permute-start(f32[4,130,1]{1,2,0:T(1,128)S(1)} %get-tuple-element.18), channel_id=1, source_target_pairs={{0,1},{1,2},{2,3},{3,4},{4,5},{5,6},{6,7},{8,9},{9,10},{10,11},{11... | collective-permute-start | bytes 6248 | tf_op jit(solution)/shard_map/ppermute | solution.py:30
  123.3 4.4 %collective-permute-start.15 = (f32[4,130,1]{1,2,0:T(1,128)S(1)}, f32[4,130,1]{1,2,0:T(1,128)S(1)}, u32[]{:S(2)}, u32[]{:S(2)}) collective-permute-start(f32[4,130,1]{1,2,0:T(1,128)S(1)} %get-tuple-element.19), channel_id=1, source_target_pairs={{1,0},{2,1},{3,2},{4,3},{5,4},{6,5},{7,6},{9,8},{10,9},{11,10},{12... | collective-permute-start | bytes 6248 | tf_op jit(solution)/shard_map/ppermute | solution.py:31
  136.6 10.2 %collective-permute-start.20 = (f32[4,1,512]{2,0,1:T(4,128)S(1)}, f32[4,1,512]{2,0,1:T(4,128)S(1)}, u32[]{:S(2)}, u32[]{:S(2)}) collective-permute-start(f32[4,1,512]{2,0,1:T(4,128)S(1)} %copy.76), channel_id=1, source_target_pairs={{0,8},{8,16},{16,24},{24,32},{32,40},{40,48},{48,56},{56,64},{64,7... | collective-permute-start | bytes 24584 | tf_op jit(solution)/shard_map/ppermute | solution.py:30
  144.6 6.5 %collective-permute-start.21 = (f32[4,1,512]{2,0,1:T(4,128)S(1)}, f32[4,1,512]{2,0,1:T(4,128)S(1)}, u32[]{:S(2)}, u32[]{:S(2)}) collective-permute-start(f32[4,1,512]{2,0,1:T(4,128)S(1)} %copy.78), channel_id=1, source_target_pairs={{8,0},{16,8},{24,16},{32,24},{40,32},{48,40},{56,48},{64,56},{72,6... | collective-permute-start | bytes 24584 | tf_op jit(solution)/shard_map/ppermute | solution.py:31
  213.1 7.9 %collective-permute-start.24 = (f32[4,1,128]{2,1,0:T(1,128)S(1)}, f32[4,1,128]{2,1,0:T(1,128)S(1)}, u32[]{:S(2)}, u32[]{:S(2)}) collective-permute-start(f32[4,1,128]{2,1,0:T(1,128)S(1)} %get-tuple-element.60), channel_id=1, source_target_pairs={{0,8},{8,16},{16,24},{24,32},{32,40},{40,48},{48,56},{56,64},{64,7... | collective-permute-start | bytes 6152 | tf_op jit(solution)/shard_map/ppermute | solution.py:30
  219.0 6.5 %collective-permute-start.25 = (f32[4,1,128]{2,1,0:T(1,128)S(1)}, f32[4,1,128]{2,1,0:T(1,128)S(1)}, u32[]{:S(2)}, u32[]{:S(2)}) collective-permute-start(f32[4,1,128]{2,1,0:T(1,128)S(1)} %get-tuple-element.61), channel_id=1, source_target_pairs={{8,0},{16,8},{24,16},{32,24},{40,32},{48,40},{56,48},{64,56},{72,6... | collective-permute-start | bytes 6152 | tf_op jit(solution)/shard_map/ppermute | solution.py:31
  228.1 5.6 %collective-permute-start.27 = (f32[4,34,1]{2,1,0:T(8,128)S(1)}, f32[4,34,1]{2,1,0:T(8,128)S(1)}, u32[]{:S(2)}, u32[]{:S(2)}) collective-permute-start(f32[4,34,1]{2,1,0:T(8,128)S(1)} %get-tuple-element.47), channel_id=1, source_target_pairs={{1,0},{2,1},{3,2},{4,3},{5,4},{6,5},{7,6},{9,8},{10,9},{11,10},{12... | collective-permute-start | bytes 1640 | tf_op jit(solution)/shard_map/ppermute | solution.py:31
  234.1 7.0 %collective-permute-start.28 = (f32[4,1,128]{2,1,0:T(1,128)S(1)}, f32[4,1,128]{2,1,0:T(1,128)S(1)}, u32[]{:S(2)}, u32[]{:S(2)}) collective-permute-start(f32[4,1,128]{2,1,0:T(1,128)S(1)} %get-tuple-element.56), channel_id=1, source_target_pairs={{0,8},{8,16},{16,24},{24,32},{32,40},{40,48},{48,56},{56,64},{64,7... | collective-permute-start | bytes 6152 | tf_op jit(solution)/shard_map/ppermute | solution.py:30
  239.1 6.5 %collective-permute-start.29 = (f32[4,1,128]{2,1,0:T(1,128)S(1)}, f32[4,1,128]{2,1,0:T(1,128)S(1)}, u32[]{:S(2)}, u32[]{:S(2)}) collective-permute-start(f32[4,1,128]{2,1,0:T(1,128)S(1)} %get-tuple-element.57), channel_id=1, source_target_pairs={{8,0},{16,8},{24,16},{32,24},{40,32},{48,40},{56,48},{64,56},{72,6... | collective-permute-start | bytes 6152 | tf_op jit(solution)/shard_map/ppermute | solution.py:31
  248.0 6.5 %collective-permute-start.31 = (f32[4,34,1]{2,1,0:T(8,128)S(1)}, f32[4,34,1]{2,1,0:T(8,128)S(1)}, u32[]{:S(2)}, u32[]{:S(2)}) collective-permute-start(f32[4,34,1]{2,1,0:T(8,128)S(1)} %get-tuple-element.45), channel_id=1, source_target_pairs={{1,0},{2,1},{3,2},{4,3},{5,4},{6,5},{7,6},{9,8},{10,9},{11,10},{12... | collective-permute-start | bytes 1640 | tf_op jit(solution)/shard_map/ppermute | solution.py:31
  254.8 7.4 %collective-permute-start.32 = (f32[4,1,128]{2,1,0:T(1,128)S(1)}, f32[4,1,128]{2,1,0:T(1,128)S(1)}, u32[]{:S(2)}, u32[]{:S(2)}) collective-permute-start(f32[4,1,128]{2,1,0:T(1,128)S(1)} %get-tuple-element.52), channel_id=1, source_target_pairs={{0,8},{8,16},{16,24},{24,32},{32,40},{40,48},{48,56},{56,64},{64,7... | collective-permute-start | bytes 6152 | tf_op jit(solution)/shard_map/ppermute | solution.py:30
  259.0 6.5 %collective-permute-start.33 = (f32[4,1,128]{2,1,0:T(1,128)S(1)}, f32[4,1,128]{2,1,0:T(1,128)S(1)}, u32[]{:S(2)}, u32[]{:S(2)}) collective-permute-start(f32[4,1,128]{2,1,0:T(1,128)S(1)} %get-tuple-element.53), channel_id=1, source_target_pairs={{8,0},{16,8},{24,16},{32,24},{40,32},{48,40},{56,48},{64,56},{72,6... | collective-permute-start | bytes 6152 | tf_op jit(solution)/shard_map/ppermute | solution.py:31
  265.6 4.4 %collective-permute-start.34 = (f32[4,34,1]{2,1,0:T(8,128)S(1)}, f32[4,34,1]{2,1,0:T(8,128)S(1)}, u32[]{:S(2)}, u32[]{:S(2)}) collective-permute-start(f32[4,34,1]{2,1,0:T(8,128)S(1)} %get-tuple-element.42), channel_id=1, source_target_pairs={{0,1},{1,2},{2,3},{3,4},{4,5},{5,6},{6,7},{8,9},{9,10},{10,11},{11... | collective-permute-start | bytes 1640 | tf_op jit(solution)/shard_map/ppermute | solution.py:30
  268.5 5.8 %collective-permute-start.35 = (f32[4,34,1]{2,1,0:T(8,128)S(1)}, f32[4,34,1]{2,1,0:T(8,128)S(1)}, u32[]{:S(2)}, u32[]{:S(2)}) collective-permute-start(f32[4,34,1]{2,1,0:T(8,128)S(1)} %get-tuple-element.43), channel_id=1, source_target_pairs={{1,0},{2,1},{3,2},{4,3},{5,4},{6,5},{7,6},{9,8},{10,9},{11,10},{12... | collective-permute-start | bytes 1640 | tf_op jit(solution)/shard_map/ppermute | solution.py:31
  (12 other events, 307.4 us)
where the time goes:
time: 278 us; the launch traced here: 275 us
  starting transfers between devices  107 us (38%)
  local copies, waits for them, and re-layouts  70.8 us (25%)
  other arithmetic  51.7 us (19%)
  waiting for transfers between devices  43.9 us (16%)
    ppermute x18, starting transfers between devices, padded(): before = lax.ppermute(last, axis, up)  78.3 us
    ppermute x18, waiting for transfers between devices, padded(): after = lax.ppermute(leading, axis, down)  43.4 us
    reshape x1, local copies, waits for them, and re-layouts, on_device(): power.reshape(layer_total, rows // BLOCK_REFINE, BLOCK_REFINE, cols // BL...  35.9 us
    ppermute x18, starting transfers between devices, padded(): after = lax.ppermute(leading, axis, down)  29.1 us
    add x3, other arithmetic, on_device(): cropped_array(voltage_grid, field_margin - step_margin) + step  23.4 us
    reduce_sum x1, other arithmetic, on_device(): warming_load = power.reshape(layer_total, rows // BLOCK_REFINE, BLOCK_REF...  12.2 us
    unnamed x24, local copies, waits for them, and re-layouts  11 us
    slice x16, local copies, waits for them, and re-layouts, padded(): last = lax.slice_in_dim(x, length - width, length, axis=dim)  10.9 us
  transfers between devices with their start and end apart: 36, of which 14 were waited for; matrix products, arithmetic and copies ran while one was open for 18% of the time, Pallas kernels for 0%

commit v1 on v0

v1 whole, which is shorter than its diff:
```python
import functools

import jax
import jax.numpy as jnp
from jax import lax
from jax.experimental import pallas as pl
from jax.experimental.pallas import tpu as pltpu
from jax.sharding import PartitionSpec as P

F32 = jnp.float32
BF16 = jnp.bfloat16
MESH = pl.DeviceIdType.MESH

LEAK = 0.2
HALF = 0.95
SIGMA = 1.0 / HALF
RHO0 = 1.0 / SIGMA
RHO1 = 1.0 / (2.0 * SIGMA - RHO0)
RHO2 = 1.0 / (2.0 * SIGMA - RHO1)
STEP_1 = (RHO1 * RHO0, 2.0 * RHO1 / HALF)
STEP_2 = (RHO2 * RHO1, 2.0 * RHO2 / HALF)
HEAT_SWEEPS = 4
DT = 0.12
GAIN = 0.0625

ROWS = 128
M0 = 8
S0 = 144
R_ALL = 184
Q0 = 16
Q_ALL = 160
H0 = 12
H_ALL = 56

DIRS = ((-1, 0), (1, 0), (0, -1), (0, 1), (-1, -1), (-1, 1), (1, -1), (1, 1))


def iota(shape, dim):
    return lax.broadcasted_iota(jnp.int32, shape, dim)


def split3(x):
    high = x.astype(BF16)
    rest = x - high.astype(F32)
    mid = rest.astype(BF16)
    low = (rest - mid.astype(F32)).astype(BF16)
    return jnp.concatenate([high, mid, low], axis=0)


def dot3(x, ones):
    rows = x.shape[0]
    y = jnp.dot(split3(x), ones, preferred_element_type=F32)
    return y[:rows] + y[rows : 2 * rows] + y[2 * rows :]


def one_zero(mask):
    return jnp.where(mask, 1.0, 0.0).astype(BF16)


class Tile:
    @staticmethod
    def left(x):
        lane = iota(x.shape, 3)
        y = pltpu.roll(x, 1, 3)
        return jnp.where(lane == 0, jnp.concatenate([y[:, 3:], y[:, :3]], axis=1), y)

    @staticmethod
    def right(x):
        lane = iota(x.shape, 3)
        y = pltpu.roll(x, 127, 3)
        return jnp.where(lane == 127, jnp.concatenate([y[:, 1:], y[:, :1]], axis=1), y)

    @staticmethod
    def tiers(vias, x):
        up = vias * x[1:]
        down = vias * x[:3]
        return jnp.concatenate([up[:1], up[1:] + down[:2], down[2:]], axis=0)

    @staticmethod
    def via_sum(vias):
        return jnp.concatenate([vias[:1], vias[1:] + vias[:2], vias[2:]], axis=0)

    @staticmethod
    def drops(vias, x):
        e = x[:3] - x[1:]
        e = vias * (e * e)
        return jnp.concatenate([e[:1], e[1:] + e[:2], e[2:]], axis=0)


class Strip:
    @staticmethod
    def left(x):
        return pltpu.roll(x, 1, 1)

    @staticmethod
    def right(x):
        return pltpu.roll(x, 127, 1)

    @staticmethod
    def tiers(vias, x):
        return vias * pltpu.roll(x, 96, 1) + pltpu.roll(vias * x, 32, 1)

    @staticmethod
    def via_sum(vias):
        return vias + pltpu.roll(vias, 32, 1)

    @staticmethod
    def drops(vias, x):
        e = x - pltpu.roll(x, 96, 1)
        e = vias * (e * e)
        return e + pltpu.roll(e, 32, 1)


def around(kind, read, mid):
    return read(-1) + read(1) + kind.left(mid) + kind.right(mid)


def sweep_first(kind, at, g, x, j, v, inv, d, w_in, w_out):
    gm, wm, xm, vm = at(g)(0), at(w_in)(0), at(x)(0), at(v)(0)
    diag = LEAK + gm * around(kind, at(g), gm) + kind.via_sum(vm)
    i = 1.0 / diag
    new = i * (at(j)(0) + gm * around(kind, at(w_in), wm) + kind.tiers(vm, xm))
    at(inv).put(i)
    at(d).put(new - xm)
    at(w_out).put(gm * new)
    return new


def sweep_next(kind, at, g, x, j, v, inv, d, w_in, w_out, weights, last):
    gm, wm, xm, vm = at(g)(0), at(w_in)(0), at(x)(0), at(v)(0)
    z = at(inv)(0) * (at(j)(0) + gm * around(kind, at(w_in), wm) + kind.tiers(vm, xm)) - xm
    step = weights[0] * at(d)(0) + weights[1] * z
    new = xm + step
    if not last:
        at(d).put(step)
        at(w_out).put(gm * new)
    return new


def node_power(kind, at, g, x, v):
    gm, xm = at(g)(0), at(x)(0)
    up = xm - at(x)(-1)
    down = xm - at(x)(1)
    right = xm - kind.right(xm)
    e = gm * kind.right(gm) * (right * right)
    rows = gm * (at(g)(-1) * (up * up) + at(g)(1) * (down * down))
    return LEAK * xm * xm + 0.5 * (rows + e + kind.left(e) + kind.drops(at(v)(0), xm))


class View:
    def __init__(self, ref, start, size):
        self.ref, self.start, self.size = ref, start, size

    def index(self, k):
        rows = pl.ds(self.start + k, self.size)
        return (slice(None),) * (len(self.ref.shape) - 2) + (rows, slice(None))

    def __call__(self, k):
        return self.ref[self.index(k)]

    def put(self, value):
        self.ref[self.index(0)] = value


def solve(kind, start, steps, size, g, x, j, v, inv, d, wa, wb, power, power_start):
    def over(body):
        if steps == 1:
            body(start, power_start)
            return

        def one(n, carry):
            off = pl.multiple_of(n * size, size)
            body(start + off, power_start + off)
            return carry

        lax.fori_loop(0, steps, one, 0)

    def first(row, _):
        at = lambda ref: View(ref, row, size)
        at(x).put(sweep_first(kind, at, g, x, j, v, inv, d, wa, wb))

    def second(row, _):
        at = lambda ref: View(ref, row, size)
        at(x).put(sweep_next(kind, at, g, x, j, v, inv, d, wb, wa, STEP_1, False))

    def third(row, _):
        at = lambda ref: View(ref, row, size)
        at(x).put(sweep_next(kind, at, g, x, j, v, inv, d, wa, wb, STEP_2, True))

    def fourth(row, out):
        at = lambda ref: View(ref, row, size)
        View(power, out, size).put(node_power(kind, at, g, x, v))

    over(first)
    over(second)
    over(third)
    over(fourth)


def pack_edges(tiers):
    rows = tiers[0][0].shape[0]
    lane = iota((rows, 128), 1)
    out = jnp.zeros((rows, 128), F32)
    for t, (first, last) in enumerate(tiers):
        base = t * 32
        low = pltpu.roll(first, (base + 4) % 128, 1)
        high = pltpu.roll(last, (base + 16 - 116) % 128, 1)
        out = jnp.where((lane >= base + 4) & (lane < base + 16), low, out)
        out = jnp.where((lane >= base + 16) & (lane < base + 28), high, out)
    return out


def with_sides(mid, from_left, from_right):
    l32 = iota(mid.shape, 1) % 32
    mid = jnp.where(l32 < 4, pltpu.roll(from_left, 104, 1), mid)
    return jnp.where(l32 >= 28, pltpu.roll(from_right, 24, 1), mid)


def kernel(
    n_row, n_col,
    v_h, a_h, t_h, vi_h, fe_h, in_h,
    xo_h, to_h,
    x, g, j, v, inv, d, wa, wb, power,
    expand, a_raw, vi_raw, fe_raw, in_raw, t_raw,
    qx, qg, qj, qv, qi, qd, qa, qb, qpower,
    ra_s, ra_r, rb_s, rb_r, cm_s, cm_r, cr_r,
    load, r2_s, r2_r, c2_s, c2_r, k2_r,
    ts, tu, hs, hu, tt, tl, ht, hl, t_out,
    in_sem, out_sem, send_sem, recv_sem, send2_sem, recv2_sem,
):
    row = lax.axis_index("row")
    col = lax.axis_index("col")

    def there(dr, dc):
        ok = None
        for cond in (
            (row > 0) if dr < 0 else (row < n_row - 1) if dr > 0 else None,
            (col > 0) if dc < 0 else (col < n_col - 1) if dc > 0 else None,
        ):
            if cond is not None:
                ok = cond if ok is None else jnp.logical_and(ok, cond)
        return ok

    def device(dr, dc):
        return {"row": row + dr, "col": col + dc}

    barrier = pltpu.get_barrier_semaphore()
    for dr, dc in DIRS:

        @pl.when(there(dr, dc))
        def _(dr=dr, dc=dc):
            pl.semaphore_signal(
                barrier, inc=1, device_id=device(dr, dc), device_id_type=MESH
            )

    copies = {}
    slot = 0

    def fetch(name, src, dst):
        nonlocal slot
        copy = pltpu.make_async_copy(src, dst, in_sem.at[slot])
        slot += 1
        copy.start()
        copies.setdefault(name, []).append(copy)

    fetch("t", t_h, t_raw)
    for name, src, dst, first in (
        ("a", a_h, a_raw, 0),
        ("x", v_h, x, M0),
        ("v", vi_h, vi_raw, 0),
        ("f", fe_h, fe_raw, 0),
        ("i", in_h, in_raw, 0),
    ):
        for b in range(4):
            fetch(
                name,
                src.at[:, :, pl.ds(128 * b, 128)],
                dst.at[:, b, pl.ds(first, ROWS), :],
            )

    def arrived(*names):
        for name in names:
            for copy in copies[name]:
                copy.wait()

    for ref in (x, g, wa, wb):
        for start in (0, M0 + ROWS, S0 + 32):
            ref[:, :, pl.ds(start, 8), :] = jnp.zeros((4, 4, 8, 128), F32)
    for ref in (qx, qg, qj, qv, qa, qb):
        for start in (0, Q0 + ROWS):
            ref[pl.ds(start, 16), :] = jnp.zeros((16, 128), F32)
    for ref in (ts, tu):
        for start in (0, 48):
            ref[:, pl.ds(start, 8), :] = jnp.zeros((4, 8, 128), F32)
    for ref in (hs, hu):
        for start in (0, 48):
            ref[pl.ds(start, 8), :] = jnp.zeros((8, 128), F32)
    for s in range(2):
        rb_s[s, pl.ds(16, 8), :] = jnp.zeros((8, 128), F32)
        r2_s[s, pl.ds(0, 8), :] = jnp.zeros((8, 128), F32)

        @pl.when(jnp.logical_not(there(*DIRS[s])))
        def _(s=s):
            ra_r[s] = jnp.zeros((15, 2, 8, 128), F32)
            rb_r[s] = jnp.zeros((40, 128), F32)
            r2_r[s] = jnp.zeros((24, 128), F32)

        @pl.when(jnp.logical_not(there(*DIRS[2 + s])))
        def _(s=s):
            cm_r[s] = jnp.zeros((96, 128), F32)
            c2_r[s] = jnp.zeros((32, 128), F32)

    for s in range(4):

        @pl.when(jnp.logical_not(there(*DIRS[4 + s])))
        def _(s=s):
            cr_r[s] = jnp.zeros((24, 128), F32)
            k2_r[s] = jnp.zeros((8, 128), F32)

    arrived("t")
    cells = jnp.exp(-0.25 * t_raw[...]).reshape(128, 128)
    wide = iota((128, 512), 1) // 4 == iota((128, 512), 0)
    fine = dot3(cells, one_zero(wide))
    for b in range(4):
        part = fine[:, 128 * b : 128 * (b + 1)].reshape(4, 32, 128)
        for k in range(4):
            expand[:, b, pl.ds(k, 32, 4), :] = part

    arrived("a", "x", "v", "f", "i")

    def prepare(n, carry):
        off = pl.multiple_of(n * 8, 8)
        at = lambda ref, first: View(ref, first + off, 8)
        adm = at(a_raw, 0)(0)
        gm = adm * lax.rsqrt(adm) * at(expand, 0)(0)
        at(g, M0).put(gm)
        at(wa, M0).put(gm * at(x, M0)(0))
        at(j, M0).put(at(fe_raw, 0)(0).astype(F32) * at(in_raw, 0)(0))
        at(v, M0).put(at(vi_raw, 0)(0).astype(F32))
        return carry

    lax.fori_loop(0, ROWS // 8, prepare, 0)

    for ref, packed, tiers in ((x, qx, 4), (g, qg, 4), (j, qj, 4), (v, qv, 3)):
        packed[pl.ds(Q0, ROWS), :] = pack_edges(
            [
                (ref[t, 0, pl.ds(M0, ROWS), :], ref[t, 3, pl.ds(M0, ROWS), :])
                for t in range(tiers)
            ]
        )
    t_edges = pack_edges([(t_raw[t], t_raw[t]) for t in range(4)])

    group = (iota((64, 128), 1) % 32) // 4
    for s, lane0 in ((0, 4), (1, 24)):
        mixed = jnp.zeros((64, 128), F32)
        for k, packed in enumerate((qx, qg, qj, qv)):
            for h in range(2):
                part = pltpu.roll(
                    packed[pl.ds(Q0 + 64 * h, 64), :], (h * 16 + k * 4 - lane0) % 128, 1
                )
                mixed = jnp.where(group == h * 4 + k, part, mixed)
        cm_s[s, pl.ds(0, 64), :] = mixed
        cm_s[s, pl.ds(64, 32), :] = t_edges
    for s, first in ((0, 0), (1, ROWS - 4)):
        for k, (ref, tiers) in enumerate(((x, 4), (g, 4), (j, 4), (v, 3))):
            for h in range(2):
                ra_s[s, pl.ds(4 * k, tiers), :, pl.ds(4 * h, 4), :] = ref[
                    :, pl.ds(2 * h, 2), pl.ds(M0 + first, 4), :
                ]
        for k, packed in enumerate((qx, qg, qj, qv)):
            rb_s[s, pl.ds(4 * k, 4), :] = packed[pl.ds(Q0 + first, 4), :]
        cell = 0 if s == 0 else 28
        rb_s[s, pl.ds(16, 4), :] = t_edges[cell : cell + 4]
        for t in range(4):
            rb_s[s, pl.ds(24 + 4 * t, 4), :] = t_raw[t, pl.ds(cell, 4), :]

    neighbours = 0
    for dr, dc in DIRS:
        neighbours = neighbours + there(dr, dc).astype(jnp.int32)
    pl.semaphore_wait(barrier, neighbours)

    def remote(src, dst, send, recv, dr, dc):
        return pltpu.make_async_remote_copy(
            src_ref=src,
            dst_ref=dst,
            send_sem=send,
            recv_sem=recv,
            device_id=device(dr, dc),
            device_id_type=MESH,
        )

    first_exchange = []
    for s in range(2):
        first_exchange.append((DIRS[s], ra_s.at[s], ra_r.at[1 - s], s, 1 - s))
        first_exchange.append((DIRS[s], rb_s.at[s], rb_r.at[1 - s], 2 + s, 3 - s))
        first_exchange.append((DIRS[2 + s], cm_s.at[s], cm_r.at[1 - s], 4 + s, 5 - s))
    for s in range(4):
        first_exchange.append(
            (DIRS[4 + s], rb_s.at[s // 2, pl.ds(0, 24)], cr_r.at[3 - s], 6 + s, 9 - s)
        )
    second_exchange = []
    for s in range(2):
        second_exchange.append((DIRS[s], r2_s.at[s], r2_r.at[1 - s], s, 1 - s))
        second_exchange.append((DIRS[2 + s], c2_s, c2_r.at[1 - s], 2 + s, 3 - s))
    for s in range(4):
        second_exchange.append(
            (DIRS[4 + s], r2_s.at[s // 2, pl.ds(0, 8)], k2_r.at[3 - s], 4 + s, 7 - s)
        )

    def start(exchange, sends, recvs):
        for (dr, dc), src, dst, a, b in exchange:

            @pl.when(there(dr, dc))
            def _(dr=dr, dc=dc, src=src, dst=dst, a=a, b=b):
                remote(src, dst, sends.at[a], recvs.at[b], dr, dc).start()

    def wait_recv(exchange, sends, recvs):
        for (dr, dc), src, dst, a, b in exchange:

            @pl.when(there(-dr, -dc))
            def _(dr=dr, dc=dc, src=src, dst=dst, a=a, b=b):
                remote(src, dst, sends.at[a], recvs.at[b], -dr, -dc).wait_recv()

    def wait_send(exchange, sends, recvs):
        for (dr, dc), src, dst, a, b in exchange:

            @pl.when(there(dr, dc))
            def _(dr=dr, dc=dc, src=src, dst=dst, a=a, b=b):
                remote(src, dst, sends.at[a], recvs.at[b], dr, dc).wait_send()

    start(first_exchange, send_sem, recv_sem)

    nodes = ((x, 4), (g, 4), (j, 4), (v, 3))
    for ref, _ in nodes:
        ref[:, :, pl.ds(S0 + 4, 12), :] = ref[:, :, pl.ds(M0, 12), :]
        ref[:, :, pl.ds(S0 + 16, 12), :] = ref[:, :, pl.ds(M0 + ROWS - 12, 12), :]

    solve(Tile, M0, ROWS // 8, 8, g, x, j, v, inv, d, wa, wb, power, 0)

    wait_recv(first_exchange, send_sem, recv_sem)

    for s, first in ((0, 0), (1, 28)):
        for k, (ref, tiers) in enumerate(nodes):
            for h in range(2):
                ref[:, pl.ds(2 * h, 2), pl.ds(S0 + first, 4), :] = ra_r[
                    s, pl.ds(4 * k, tiers), :, pl.ds(4 * h, 4), :
                ]
    strip = pl.ds(S0, 32)
    wa[:, :, strip, :] = g[:, :, strip, :] * x[:, :, strip, :]
    solve(Tile, S0, 4, 8, g, x, j, v, inv, d, wa, wb, power, ROWS)

    l32 = iota((64, 128), 1) % 32
    for k, packed in enumerate((qx, qg, qj, qv)):
        for s, first in ((0, Q0 - 4), (1, Q0 + ROWS)):
            part = pl.ds(4 * k, 4)
            packed[pl.ds(first, 4), :] = with_sides(
                rb_r[s, part, :], cr_r[2 * s, part, :], cr_r[2 * s + 1, part, :]
            )
        for h in range(2):
            rows = pl.ds(Q0 + 64 * h, 64)
            lane0 = h * 16 + k * 4
            mid = packed[rows, :]
            mid = jnp.where(
                l32 < 4, pltpu.roll(cm_r[0, pl.ds(0, 64), :], -lane0 % 128, 1), mid
            )
            packed[rows, :] = jnp.where(
                l32 >= 28, pltpu.roll(cm_r[1, pl.ds(0, 64), :], (28 - lane0) % 128, 1), mid
            )
    strip = pl.ds(8, 144)
    qa[strip, :] = qg[strip, :] * qx[strip, :]
    solve(Strip, 8, 1, 144, qg, qx, qj, qv, qi, qd, qa, qb, qpower, 8)

    x[:, :, pl.ds(M0, 4), :] = x[:, :, pl.ds(S0 + 4, 4), :]
    x[:, :, pl.ds(M0 + ROWS - 4, 4), :] = x[:, :, pl.ds(S0 + 24, 4), :]
    power[:, :, pl.ds(0, 4), :] = power[:, :, pl.ds(ROWS + 4, 4), :]
    power[:, :, pl.ds(ROWS - 4, 4), :] = power[:, :, pl.ds(ROWS + 24, 4), :]
    lane = iota((ROWS, 128), 1)
    sides = qx[pl.ds(Q0, ROWS), :]
    tile = pl.ds(M0, ROWS)
    for t in range(4):
        x[t, 0, tile, :] = jnp.where(
            lane < 4, pltpu.roll(sides, (-4 - 32 * t) % 128, 1), x[t, 0, tile, :]
        )
        x[t, 3, tile, :] = jnp.where(
            lane >= 124, pltpu.roll(sides, (100 - 32 * t) % 128, 1), x[t, 3, tile, :]
        )
    out_copies = []
    for b in range(4):
        copy = pltpu.make_async_copy(
            x.at[:, b, tile, :], xo_h.at[:, :, pl.ds(128 * b, 128)], out_sem.at[b]
        )
        copy.start()
        out_copies.append(copy)

    sums = power[:, :, pl.ds(0, 32, 4), :]
    edge_sums = qpower[pl.ds(Q0, 32, 4), :]
    for k in range(1, 4):
        sums = sums + power[:, :, pl.ds(k, 32, 4), :]
        edge_sums = edge_sums + qpower[pl.ds(Q0 + k, 32, 4), :]
    total = jnp.zeros((128, 128), F32)
    for h in range(2):
        node, cell = iota((256, 128), 0), iota((256, 128), 1)
        pick = (node // 4 + 64 * h == cell) & (cell > 0) & (cell < 127)
        both = jnp.concatenate(
            [sums[:, 2 * h].reshape(128, 128), sums[:, 2 * h + 1].reshape(128, 128)], axis=1
        )
        total = total + dot3(both, one_zero(pick))
    lane, cell = iota((128, 512), 0), iota((128, 512), 1)
    base = (cell // 128) * 32
    pick = ((cell % 128 == 0) & (lane >= base + 4) & (lane < base + 8)) | (
        (cell % 128 == 127) & (lane >= base + 24) & (lane < base + 28)
    )
    edge_cells = dot3(edge_sums, one_zero(pick))
    for t in range(4):
        load[t] = GAIN * (
            total[32 * t : 32 * (t + 1)] + edge_cells[:, 128 * t : 128 * (t + 1)]
        )

    l_edges = pack_edges([(load[t], load[t]) for t in range(4)])
    c2_s[...] = l_edges
    for s, cell in ((0, 0), (1, 28)):
        r2_s[s, pl.ds(0, 4), :] = l_edges[cell : cell + 4]
        for t in range(4):
            r2_s[s, pl.ds(8 + 4 * t, 4), :] = load[t, pl.ds(cell, 4), :]
    start(second_exchange, send2_sem, recv2_sem)

    for t in range(4):
        tt[t, pl.ds(0, 4), :] = rb_r[0, pl.ds(24 + 4 * t, 4), :]
        tt[t, pl.ds(4, 32), :] = t_raw[t]
        tt[t, pl.ds(36, 4), :] = rb_r[1, pl.ds(24 + 4 * t, 4), :]
    cells = pl.ds(64, 32)
    edge = pl.ds(16, 4)
    ht[pl.ds(0, 4), :] = with_sides(rb_r[0, edge, :], cr_r[0, edge, :], cr_r[1, edge, :])
    ht[pl.ds(4, 32), :] = with_sides(t_edges, cm_r[0, cells, :], cm_r[1, cells, :])
    ht[pl.ds(36, 4), :] = with_sides(rb_r[1, edge, :], cr_r[2, edge, :], cr_r[3, edge, :])

    r = iota((40, 128), 0)
    l32 = iota((40, 128), 1) % 32
    rows_in = ((r >= 4) | (row > 0)) & ((r < 36) | (row < n_row - 1))
    cols_in = ((l32 >= 4) | (col > 0)) & ((l32 < 28) | (col < n_col - 1))
    row_mask = jnp.where(rows_in, 1.0, 0.0).astype(F32)
    all_mask = jnp.where(rows_in & cols_in, 1.0, 0.0).astype(F32)
    tier = iota((40, 128), 1) // 32
    not_first = jnp.where(tier > 0, 1.0, 0.0).astype(F32)
    not_last = jnp.where(tier < 3, 1.0, 0.0).astype(F32)

    def increment_tile(theta):
        s = jnp.exp(-0.15 * theta) * row_mask
        u = s * theta
        ts[:, pl.ds(8, 40), :] = s
        tu[:, pl.ds(8, 40), :] = u
        near_s = ts[:, pl.ds(7, 40), :] + ts[:, pl.ds(9, 40), :]
        near_u = tu[:, pl.ds(7, 40), :] + tu[:, pl.ds(9, 40), :]
        near_s = near_s + pltpu.roll(s, 1, 2) + pltpu.roll(s, 127, 2)
        near_u = near_u + pltpu.roll(u, 1, 2) + pltpu.roll(u, 127, 2)
        flux = s * (near_u - theta * near_s)
        vert = jnp.concatenate(
            [
                theta[1:2] - theta[0:1],
                theta[0:2] + theta[2:4] - 2.0 * theta[1:3],
                theta[2:3] - 2.0 * theta[3:4],
            ],
            axis=0,
        )
        return flux + vert

    def increment_strip(theta):
        s = jnp.exp(-0.15 * theta) * all_mask
        u = s * theta
        hs[pl.ds(8, 40), :] = s
        hu[pl.ds(8, 40), :] = u
        near_s = hs[pl.ds(7, 40), :] + hs[pl.ds(9, 40), :]
        near_u = hu[pl.ds(7, 40), :] + hu[pl.ds(9, 40), :]
        near_s = near_s + pltpu.roll(s, 1, 1) + pltpu.roll(s, 127, 1)
        near_u = near_u + pltpu.roll(u, 1, 1) + pltpu.roll(u, 127, 1)
        flux = s * (near_u - theta * near_s)
        vert = (
            not_last * pltpu.roll(theta, 96, 1)
            + not_first * pltpu.roll(theta, 32, 1)
            - (1.0 + not_first) * theta
        )
        return flux + vert

    theta, side = tt[...], ht[...]
    gain, side_gain = increment_tile(theta), increment_strip(side)

    wait_recv(second_exchange, send2_sem, recv2_sem)
    for t in range(4):
        tl[t, pl.ds(0, 4), :] = r2_r[0, pl.ds(8 + 4 * t, 4), :]
        tl[t, pl.ds(4, 32), :] = load[t]
        tl[t, pl.ds(36, 4), :] = r2_r[1, pl.ds(8 + 4 * t, 4), :]
    edge = pl.ds(0, 4)
    hl[pl.ds(0, 4), :] = with_sides(r2_r[0, edge, :], k2_r[0, edge, :], k2_r[1, edge, :])
    hl[pl.ds(4, 32), :] = with_sides(l_edges, c2_r[0], c2_r[1])
    hl[pl.ds(36, 4), :] = with_sides(r2_r[1, edge, :], k2_r[2, edge, :], k2_r[3, edge, :])
    heat, side_heat = tl[...], hl[...]

    for sweep in range(HEAT_SWEEPS):
        if sweep > 0:
            gain, side_gain = increment_tile(theta), increment_strip(side)
        theta = theta + DT * (gain + heat)
        side = side + DT * (side_gain + side_heat)

    tt[...] = theta
    ht[...] = side
    lane = iota((32, 128), 1)
    sides = ht[pl.ds(4, 32), :]
    for t in range(4):
        mid = tt[t, pl.ds(4, 32), :]
        mid = jnp.where(lane < 4, pltpu.roll(sides, (-4 - 32 * t) % 128, 1), mid)
        mid = jnp.where(lane >= 124, pltpu.roll(sides, (100 - 32 * t) % 128, 1), mid)
        t_out[t] = mid
    copy = pltpu.make_async_copy(t_out, to_h, out_sem.at[4])
    copy.start()
    out_copies.append(copy)

    wait_send(first_exchange, send_sem, recv_sem)
    wait_send(second_exchange, send2_sem, recv2_sem)
    for copy in out_copies:
        copy.wait()


def vmem(*shape, dtype=F32):
    return pltpu.VMEM(shape, dtype)


def on_device(n_row, n_col, *args):
    node = (4, 4, R_ALL, 128)
    raw = (4, 4, ROWS, 128)
    strip = (Q_ALL, 128)
    scratch = [
        vmem(*node), vmem(*node), vmem(*node), vmem(3, *node[1:]),
        vmem(*node), vmem(*node), vmem(*node), vmem(*node),
        vmem(4, 4, ROWS + 32, 128),
        vmem(*raw), vmem(*raw), vmem(3, *raw[1:], dtype=jnp.int32),
        vmem(*raw, dtype=jnp.int32), vmem(*raw), vmem(4, 32, 128),
        *[vmem(*strip) for _ in range(9)],
        vmem(2, 15, 2, 8, 128), vmem(2, 15, 2, 8, 128),
        vmem(2, 40, 128), vmem(2, 40, 128),
        vmem(2, 96, 128), vmem(2, 96, 128),
        vmem(4, 24, 128),
        vmem(4, 32, 128),
        vmem(2, 24, 128), vmem(2, 24, 128),
        vmem(32, 128), vmem(2, 32, 128),
        vmem(4, 8, 128),
        vmem(4, H_ALL, 128), vmem(4, H_ALL, 128), vmem(H_ALL, 128), vmem(H_ALL, 128),
        vmem(4, 40, 128), vmem(4, 40, 128), vmem(40, 128), vmem(40, 128),
        vmem(4, 32, 128),
        pltpu.SemaphoreType.DMA((21,)),
        pltpu.SemaphoreType.DMA((5,)),
        pltpu.SemaphoreType.DMA((10,)),
        pltpu.SemaphoreType.DMA((10,)),
        pltpu.SemaphoreType.DMA((8,)),
        pltpu.SemaphoreType.DMA((8,)),
    ]
    hbm = pl.BlockSpec(memory_space=pl.ANY)
    return pl.pallas_call(
        functools.partial(kernel, n_row, n_col),
        out_shape=(
            jax.ShapeDtypeStruct((4, ROWS, 512), F32),
            jax.ShapeDtypeStruct((4, 32, 128), F32),
        ),
        in_specs=[hbm] * 6,
        out_specs=(hbm, hbm),
        scratch_shapes=scratch,
        compiler_params=pltpu.CompilerParams(
            collective_id=0,
            has_side_effects=True,
            vmem_limit_bytes=56 * 1024 * 1024,
        ),
    )(*args)


def solution(mesh):
    spec = P(None, "row", "col")
    return jax.shard_map(
        functools.partial(on_device, mesh.shape["row"], mesh.shape["col"]),
        mesh=mesh,
        in_specs=(spec,) * 6,
        out_specs=(spec, spec),
        check_vma=False,
    )
```

time: 278 us -> 29.1 us (0.10)
  starting transfers between devices: 107 us -> 0 us
  local copies, waits for them, and re-layouts: 70.8 us -> 2.93 us
  other arithmetic: 51.7 us -> 0 us
  waiting for transfers between devices: 43.9 us -> 0 us
  Pallas kernels: 0 us -> 25.4 us
    ppermute x36 -> x0, starting transfers between devices: 107 us -> none  [the longest x18 78.3 us: padded(): before = lax.ppermute(last, axis, up)]
    ppermute x36 -> x0, waiting for transfers between devices: 43.9 us -> none  [the longest x18 43.4 us: padded(): after = lax.ppermute(leading, axis, down)]
    reshape x1 -> x0, local copies, waits for them, and re-layouts: 35.9 us -> none  [on_device(): power.reshape(layer_total, rows // BLOCK_REFINE, BLOCK_REFINE, cols // BL...]
    add x8 -> x0, other arithmetic: 28.7 us -> none  [the longest x3 23.4 us: on_device(): cropped_array(voltage_grid, field_margin - step_margin) + step]
    pallas_call x0 -> x1, Pallas kernels: none -> 25.4 us  [on_device(): pl.pallas_call(functools.partial(kernel, n_row, n_col), out_shape=(jax.Sh...]
    slice x21 -> x0, local copies, waits for them, and re-layouts: 12.6 us -> none  [the longest x16 10.9 us: padded(): last = lax.slice_in_dim(x, length - width, length, axis=dim)]
    reduce_sum x1 -> x0, other arithmetic: 12.2 us -> none  [on_device(): warming_load = power.reshape(layer_total, rows // BLOCK_REFINE, BLOCK_REF...]
    ppermute x10 -> x0, local copies, waits for them, and re-layouts: 10.6 us -> none  [the longest x5 6.77 us: padded(): after = lax.ppermute(leading, axis, down)]
  transfers between devices with their start and end apart: 36 -> 0, of which waited for: 14 -> 0; matrix products, arithmetic and copies ran while one was open for 18% -> 0% of each run, Pallas kernels for 0% -> 0%
where the time goes in v1:
time: 29.1 us; the launch traced here: 29 us
  Pallas kernels  25.4 us (87%)
  local copies, waits for them, and re-layouts  2.93 us (10%)
  between operations  0.65 us (2%)
    pallas_call x1, Pallas kernels, on_device(): pl.pallas_call(functools.partial(kernel, n_row, n_col), out_shape=(jax.Sh...  25.4 us
    unnamed x4, local copies, waits for them, and re-layouts  2.93 us

profile of v1, /device:TPU:1, one launch (start us, length us, event | category | flops | bytes accessed | tf_op | source)
XLA Modules:
  0.0 29.0 jit_solution(9678664146678619284)
XLA Ops:
  0.6 25.4 %shard_map.77 = (f32[4,128,512]{2,1,0:T(8,128)}, f32[4,32,128]{2,1,0:T(8,128)}) custom-call(f32[4,128,512]{2,1,0:T(8,128)} %v_h.1, f32[4,128,512]{2,1,0:T(8,128)} %a_h.1, f32[4,32,128]{2,1,0:T(8,128)} %t_h.1, s32[3,128,512]{2,1,0:T(8,128)} %vi_h.1, s32[4,128,512]{2,1,0:T(8,128)} %fe_h.1, f32[4,128,512]{2,1,0:T(8,128)} %in_h.1), custom_call_target="tpu_custom_call" | custom-call | tf_op jit(solution)/shard_map/pallas_call | solution.py:657
  26.1 0.0 copy-start
  26.1 2.3 %copy.10 = f32[4,128,512]{2,1,0:T(8,128)} copy(f32[4,128,512]{2,1,0:T(8,128)} %get-tuple-element.4) | data formatting | bytes 2097152
  28.4 0.0 copy-done
  28.4 0.6 %copy.11 = f32[4,32,128]{2,1,0:T(8,128)} copy(f32[4,32,128]{2,1,0:T(8,128)S(1)} %copy-done) | data formatting | bytes 131072
Async XLA Ops:
  26.1 2.3 %copy-start = (f32[4,32,128]{2,1,0:T(8,128)S(1)}, f32[4,32,128]{2,1,0:T(8,128)}, u32[]{:S(2)}) copy-start(f32[4,32,128]{2,1,0:T(8,128)} %get-tuple-element.5) | copy-start | bytes 196612
